TPU v7x, 32 devices: a whole 2x2x4 slice. The times are simulated.
32 devices in a mesh: wave: 16 (over z, x, core), level: 2 (over y).
Axes of the slice: x: 2, y: 2, z: 4, core: 2. Of those that a mesh axis runs over, the one named last changes fastest.
Arguments:
- state: float32 [4, 64, 256, 2, 256], P(None, 'level', 'wave'), may hold values from -0.02 to 0.02
- legendre: float32 [256, 384, 256], P('wave'), may hold values from -6 to 6
- lat_weight: float32 [384], P('wave'), may hold values from 0.8 to 2
- modes: float32 [64, 64], replicated, may hold values from -1 to 1, as said below
- mode_rates: float32 [64], replicated, may hold values from 1e-05 to 0.003
- diffusion: float32 [4], replicated, may hold values from 0.3 to 3
- norm_gain: float32 [256], replicated, may hold values from 0.5 to 1.5
- w_first: bfloat16 [1024, 256], replicated, may hold values from -0.375 to 0.375
- b_first: float32 [1024], replicated, may hold values from -3 to 3
- w_second: bfloat16 [1024, 1024], replicated, may hold values from -0.1875 to 0.1875
- b_second: float32 [1024], replicated, may hold values from -3 to 3
- w_third: bfloat16 [256, 1024], replicated, may hold values from -0.1875 to 0.1875
- b_third: float32 [256], replicated, may hold values from -1.2 to 1.2
Outputs:
- next_state: float32 [4, 64, 256, 2, 256], P(None, 'level', 'wave')
Inputs may be any that keep to these rules, and one draw needn't show every extreme that they name: `modes`: orthogonal: its transpose is its inverse.
All inputs are finite; a program needn't handle non-finite values.
Results may differ from a plain program's by a relative error of at most 0.0011.
Values may be sent and summed in bfloat16 or wider, within the bound.
A program may use at most 192 MiB of HBM per device.

v0:
```python
import jax
import jax.numpy as jnp
from jax import lax
from jax.sharding import PartitionSpec as P

M = 256
LAT = 384
LON = 768


highest = lax.Precision.HIGHEST
norm_eps = 1e-06


def phase_angles(waves, longitudes):
    wave_idx = jnp.arange(waves, dtype=jnp.int32)
    lon_idx = jnp.arange(longitudes, dtype=jnp.int32)
    phase_turns = wave_idx[:, None] * lon_idx[None, :] % longitudes
    return (2.0 * jnp.pi / longitudes * phase_turns.astype(jnp.float32), wave_idx)


def synthesis_table(waves, longitudes):
    angle_table, wave_idx = phase_angles(waves, longitudes)
    factor = jnp.where(wave_idx == 0, 1.0, 2.0).astype(jnp.float32)[:, None]
    return jnp.stack([factor * jnp.cos(angle_table), -factor * jnp.sin(angle_table)], axis=1)


def analysis_table(waves, longitudes):
    angle_table, wave_idx = phase_angles(waves, longitudes)
    flipped = angle_table.T
    return jnp.stack([jnp.cos(flipped), -jnp.sin(flipped)], axis=2) / longitudes


def column_physics(columns, norm_gain, w_first, b_first, w_second, b_second, w_third, b_third):
    values = columns.astype(jnp.float32)
    inverse_rms = lax.rsqrt(jnp.mean(values * values, axis=0, keepdims=True) + norm_eps)
    normed = (values * inverse_rms * norm_gain[:, None]).astype(jnp.bfloat16)
    hidden_one = jax.nn.gelu(
        jnp.dot(w_first, normed, preferred_element_type=jnp.float32) + b_first[:, None]
    ).astype(jnp.bfloat16)
    hidden_two = jax.nn.gelu(
        jnp.dot(w_second, hidden_one, preferred_element_type=jnp.float32) + b_second[:, None]
    ).astype(jnp.bfloat16)
    return (
        jnp.dot(w_third, hidden_two, preferred_element_type=jnp.float32) + b_third[:, None]
    ).astype(jnp.bfloat16)


def body(
    state,
    legendre,
    lat_weight,
    modes,
    mode_rates,
    diffusion,
    norm_gain,
    w_first,
    b_first,
    w_second,
    b_second,
    w_third,
    b_third,
):
    fields = state.shape[0]
    lev_dev = state.shape[1]
    m_dev = state.shape[2]
    complex_parts = state.shape[3]
    degrees = state.shape[4]
    levels = modes.shape[0]
    wave_count = lax.axis_size("wave")
    lat_dev = LAT // wave_count
    wave_global = lax.axis_index("wave") * m_dev + jnp.arange(m_dev, dtype=jnp.int32)
    degree_index = wave_global[:, None] + jnp.arange(degrees, dtype=jnp.int32)[None, :]
    kept_mask = (degree_index < M).astype(jnp.float32)
    kept_basis = legendre * kept_mask[:, None, :]
    basis_blocks = kept_basis.reshape(m_dev, wave_count, lat_dev, degrees)
    inverse_tab = synthesis_table(M, LON).reshape(wave_count, m_dev, complex_parts, LON)
    forward_tab = analysis_table(M, LON).reshape(LON, wave_count, m_dev, complex_parts)
    pieces = []
    for field_index in range(fields):
        band_coeffs = jnp.einsum(
            "lmcj,mwaj->wlcma", state[field_index], basis_blocks, precision=highest
        )
        exchanged = lax.all_to_all(
            band_coeffs.reshape(wave_count, -1), "wave", split_axis=0, concat_axis=0, tiled=True
        )
        shaped = exchanged.reshape(wave_count, lev_dev, complex_parts, m_dev, lat_dev)
        pieces.append(jnp.einsum("wlcma,wmco->lao", shaped, inverse_tab, precision=highest))
    grid_field = jnp.stack(pieces)
    grid_low = grid_field.astype(jnp.bfloat16)
    slab = grid_low.reshape(fields, lev_dev, lat_dev * LON)
    columns = lax.all_to_all(slab, "level", split_axis=2, concat_axis=1, tiled=True)
    col_count = columns.shape[2]
    tendency = column_physics(
        columns.reshape(fields * levels, col_count),
        norm_gain,
        w_first,
        b_first,
        w_second,
        b_second,
        w_third,
        b_third,
    )
    tendency = tendency.reshape(fields, levels, col_count)
    returned = lax.all_to_all(tendency, "level", split_axis=1, concat_axis=2, tiled=True).reshape(
        fields, lev_dev, lat_dev, LON
    )
    updated = (grid_field + returned.astype(jnp.float32)) * lat_weight[None, None, :, None]
    field_parts = []
    for field_index in range(fields):
        wave_coeffs = jnp.einsum(
            "lao,owmc->wlcma", updated[field_index], forward_tab, precision=highest
        )
        exchanged = lax.all_to_all(
            wave_coeffs.reshape(wave_count, -1), "wave", split_axis=0, concat_axis=0, tiled=True
        )
        shaped = exchanged.reshape(wave_count, lev_dev, complex_parts, m_dev, lat_dev)
        field_parts.append(jnp.einsum("wlcma,mwaj->lmcj", shaped, basis_blocks, precision=highest))
    spectral = jnp.stack(field_parts)
    growth = (degree_index * (degree_index + 1)).astype(jnp.float32)
    divisor = 1.0 + mode_rates[:, None, None, None] * growth[None, :, None, :]
    divisor = jnp.broadcast_to(divisor, (levels, m_dev, complex_parts, degrees)).reshape(levels, -1)
    divergence = spectral[1].reshape(lev_dev, -1)
    lev_start = lax.axis_index("level") * lev_dev
    own_rows = lax.dynamic_slice_in_dim(modes, lev_start, lev_dev, 0)
    amplitude = jnp.dot(
        modes.T,
        lax.all_gather(divergence, "level", axis=0, tiled=True),
        precision=highest,
        preferred_element_type=jnp.float32,
    )
    amplitude = amplitude / divisor
    solved = jnp.dot(own_rows, amplitude, precision=highest, preferred_element_type=jnp.float32)
    solved = solved.reshape(lev_dev, m_dev, complex_parts, degrees)
    combined = jnp.concatenate([spectral[:1], solved[None], spectral[2:]], axis=0)
    scaled_growth = growth / (M * (M - 1))
    damping = 1.0 + diffusion[:, None, None] * (scaled_growth * scaled_growth)[None]
    return combined / damping[:, None, :, None, :]


def solution(mesh):
    in_specs = (
        P(None, "level", "wave", None, None),
        P("wave", None, None),
        P("wave"),
        P(),
        P(),
        P(),
        P(),
        P(),
        P(),
        P(),
        P(),
        P(),
        P(),
    )
    out_specs = P(None, "level", "wave", None, None)
    return jax.shard_map(body, mesh=mesh, in_specs=in_specs, out_specs=out_specs, check_vma=False)
```

profile of v0, /device:TPU:0, one launch (start us, length us, event | category | flops | bytes accessed | tf_op | source)
XLA Modules:
  0.0 1028.1 jit_solution(9725989835272598431)
XLA Ops:
  24.2 10.3 %copy.193 = f32[16,32,2,16,24]{4,3,2,1,0:T(8,128)} copy(f32[16,32,2,16,24]{1,4,2,0,3:T(8,128)} %convolution_bitcast_fusion.8) | data formatting | bytes 3145728 | tf_op jit(solution)/shard_map/lmcj,mwaj->wlcma/transpose | solution.py:81
  34.5 9.1 all_to_all.80
  51.6 9.9 convolution_bitcast_fusion.7
  61.5 10.3 %copy.196 = f32[16,32,2,16,24]{4,3,2,1,0:T(8,128)} copy(f32[16,32,2,16,24]{1,4,2,0,3:T(8,128)} %convolution_bitcast_fusion.7) | data formatting | bytes 3145728 | tf_op jit(solution)/shard_map/lmcj,mwaj->wlcma/transpose | solution.py:81
  71.8 9.1 all_to_all.81
  92.7 9.9 convolution_bitcast_fusion.6
  102.5 10.3 %copy.199 = f32[16,32,2,16,24]{4,3,2,1,0:T(8,128)} copy(f32[16,32,2,16,24]{1,4,2,0,3:T(8,128)} %convolution_bitcast_fusion.6) | data formatting | bytes 3145728 | tf_op jit(solution)/shard_map/lmcj,mwaj->wlcma/transpose | solution.py:81
  112.8 9.2 all_to_all.82
  124.6 9.2 all-to-all-start.2
  133.7 12.3 %convolution_bitcast_fusion.5 = f32[16,32,2,16,24]{1,4,2,0,3:T(8,128)} fusion(f32[16,16,24,256,1]{3,2,4,1,0:T(8,128)} %bitcast.214, f32[1,32,16,2,256]{4,3,2,1,0:T(2,128)S(1)} %get-tuple-element.12), kind=kOutput, calls=%fused_computation.49 | convolution fusion | flops 1207959552 | bytes 8912896 | tf_op jit(solution)/shard_map/lmcj,mwaj->wlcma/dot_general | solution.py:81
  146.1 10.3 %copy.202 = f32[16,32,2,16,24]{4,3,2,1,0:T(8,128)} copy(f32[16,32,2,16,24]{1,4,2,0,3:T(8,128)} %convolution_bitcast_fusion.5) | data formatting | bytes 3145728 | tf_op jit(solution)/shard_map/lmcj,mwaj->wlcma/transpose | solution.py:81
  165.6 9.2 all-to-all-start.3
  186.1 9.2 reshape.350
  195.3 18.1 %bitcast_convert_fusion.3 = (bf16[32,24,768]{2,1,0:T(8,128)(2,1)}, f32[32,24,768,1,1]{2,1,3,0,4:T(8,128)}) fusion(f32[16,32,2,16,24]{4,3,2,1,0:T(8,128)} %reshape.350, f32[16,16,1,768]{3,1,2,0:T(8,128)} %get-tuple-element.16, f32[16,16,1,768]{3,1,2,0:T(8,128)S(1)} %get-tuple-element.15), kind=kOutput, calls=%fused_computation.64 | convolution fusion | flops 3624861696 | bytes 6684672 | tf_op jit(solution)/shard_map/wlcma,wmco->lao/dot_general | solution.py:88
  222.2 9.6 reshape.351
  231.8 17.8 %bitcast_convert_fusion.2 = (bf16[32,24,768]{2,1,0:T(8,128)(2,1)}, f32[32,24,768,1,1]{2,1,3,0,4:T(8,128)}) fusion(f32[16,32,2,16,24]{4,3,2,1,0:T(8,128)} %reshape.351, f32[16,16,1,768]{3,1,2,0:T(8,128)} %get-tuple-element.16, f32[16,16,1,768]{3,1,2,0:T(8,128)S(1)} %get-tuple-element.15), kind=kOutput, calls=%fused_computation.63 | convolution fusion | flops 3624861696 | bytes 6684672 | tf_op jit(solution)/shard_map/wlcma,wmco->lao/dot_general | solution.py:88
  258.6 9.2 reshape.352
  267.8 17.8 %bitcast_convert_fusion.1 = (bf16[32,24,768]{2,1,0:T(8,128)(2,1)}, f32[32,24,768,1,1]{2,1,3,0,4:T(8,128)}) fusion(f32[16,32,2,16,24]{4,3,2,1,0:T(8,128)} %reshape.352, f32[16,16,1,768]{3,1,2,0:T(8,128)} %get-tuple-element.16, f32[16,16,1,768]{3,1,2,0:T(8,128)S(1)} %get-tuple-element.15), kind=kOutput, calls=%fused_computation.62 | convolution fusion | flops 3624861696 | bytes 6684672 | tf_op jit(solution)/shard_map/wlcma,wmco->lao/dot_general | solution.py:88
  294.6 9.2 reshape.353
  303.8 17.8 %bitcast_convert_fusion = (bf16[32,24,768]{2,1,0:T(8,128)(2,1)}, f32[32,24,768,1,1]{2,1,3,0,4:T(8,128)}) fusion(f32[16,32,2,16,24]{4,3,2,1,0:T(8,128)} %reshape.353, f32[16,16,1,768]{3,1,2,0:T(8,128)} %get-tuple-element.16, f32[16,16,1,768]{3,1,2,0:T(8,128)S(1)} %get-tuple-element.15), kind=kOutput, calls=%fused_computation.61 | convolution fusion | flops 3624861696 | bytes 6684672 | tf_op jit(solution)/shard_map/wlcma,wmco->lao/dot_general | solution.py:88
  327.2 22.5 %copy.204 = bf16[4,32,18432]{1,0,2:T(4,128)(2,1)} copy(bf16[4,32,18432]{2,1,0:T(8,128)(2,1)} %pad_maximum_fusion) | data formatting | bytes 9437184 | tf_op jit(solution)/shard_map/stack | solution.py:89
  349.7 28.2 %reshape.391 = bf16[2,2,589824]{2,1,0:T(2,128)(2,1)} reshape(bf16[18432,4,32]{2,1,0:T(4,128)(2,1)} %bitcast.221) | data formatting | bytes 9437184
  377.9 61.8 %all_to_all.98 = bf16[2,2,589824]{2,1,0:T(2,128)(2,1)} all-to-all(bf16[2,2,589824]{2,1,0:T(2,128)(2,1)} %reshape.391), channel_id=1, replica_groups=mesh['wave'=16,'level'=2] {'level'}, dimensions={0} | all-to-all | bytes 9437184 | tf_op jit(solution)/shard_map/all_to_all | solution.py:92
  439.7 20.3 %reshape.392 = bf16[18432,4,32]{2,1,0:T(4,128)(2,1)} reshape(bf16[2,2,589824]{2,1,0:T(2,128)(2,1)} %all_to_all.98) | data formatting | bytes 9437184
  460.0 22.8 %copy.205 = bf16[4,32,18432]{2,1,0:T(8,128)(2,1)} copy(bf16[4,32,18432]{1,0,2:T(4,128)(2,1)} %bitcast.222) | data formatting | bytes 9437184 | tf_op jit(solution)/shard_map/all_to_all | solution.py:92
  482.9 12.7 %reshape.362 = f32[4,32,2,9216]{3,2,1,0:T(2,128)} reshape(bf16[4,32,18432]{2,1,0:T(8,128)(2,1)} %copy.205) | data formatting | bytes 14155776 | tf_op jit(solution)/shard_map/convert_element_type | solution.py:35
  498.9 10.2 copy.206
  514.3 19.3 %fusion.7.clone.4 = bf16[1024,9216]{0,1:T(8,128)(2,1)} fusion(bf16[256,9216]{1,0:T(8,128)(2,1)S(1)} %fusion.24, bf16[1024,256]{1,0:T(8,128)(2,1)S(1)} %copy-done.17, f32[1024]{0:T(1024)S(1)} %copy-done.19), kind=kOutput, calls=%fused_computation.9.clone.clone.clone.1 | convolution fusion | flops 4926210048 | bytes 24121344 | tf_op jit(solution)/shard_map/dot_general | solution.py:39
  533.6 38.6 %fusion.15 = bf16[1024,9216]{0,1:T(8,128)(2,1)} fusion(bf16[1024,1024]{1,0:T(8,128)(2,1)S(1)} %copy-done, f32[1024]{0:T(1024)S(1)} %copy-done.20, bf16[1024,9216]{0,1:T(8,128)(2,1)} %fusion.7.clone.4), kind=kOutput, calls=%fused_computation.17 | convolution fusion | flops 19421724672 | bytes 39849984 | tf_op jit(solution)/shard_map/dot_general | solution.py:42
  572.2 19.2 %fusion.21 = bf16[9216,256]{0,1:T(8,128)(2,1)S(1)} fusion(bf16[1024,9216]{0,1:T(8,128)(2,1)} %fusion.15, bf16[256,1024]{1,0:T(8,128)(2,1)S(1)} %copy-done.18, f32[256]{0:T(256)S(1)} %copy-done.21), kind=kOutput, calls=%fused_computation.24 | convolution fusion | flops 4836556800 | bytes 24118272 | tf_op jit(solution)/shard_map/dot_general | solution.py:45
  606.5 49.7 %all-to-all-done.5 = bf16[4,64,9216]{2,0,1:T(4,128)(2,1)} async-done(((bf16[4,64,9216]{2,0,1:T(4,128)(2,1)}), bf16[4,64,9216]{2,0,1:T(4,128)(2,1)}, u32[]{:S(2)}, u32[]{:S(2)}) %all-to-all-start.5) | async-done | bytes 4718624 | tf_op jit(solution)/shard_map/all_to_all | solution.py:105
  669.3 13.1 %reshape.361 = f32[4,32,24,768]{3,2,1,0:T(8,128)} reshape(f32[4,32,2,9216]{3,2,1,0:T(2,128)} %copy.209) | data formatting | bytes 18874368 | tf_op jit(solution)/shard_map/convert_element_type | solution.py:108
  692.8 17.0 %convolution_bitcast_fusion.3 = f32[16,32,2,16,24]{1,3,4,2,0:T(8,128)} fusion(f32[32,24,768,1,1]{2,1,0,4,3:T(8,128)S(1)} %get-tuple-element.8, f32[768,16,16,1]{0,2,3,1:T(8,128)S(1)} %get-tuple-element.14, f32[768,16,16,1]{0,2,3,1:T(8,128)S(1)} %get-tuple-element.13), kind=kOutput, calls=%fused_computation.47 | convolution fusion | flops 3624665088 | bytes 5505024 | tf_op jit(solution)/shard_map/lao,owmc->wlcma/dot_general | solution.py:111
  709.7 10.6 %copy.215 = f32[16,32,2,16,24]{4,3,2,1,0:T(8,128)} copy(f32[16,32,2,16,24]{1,3,4,2,0:T(8,128)} %convolution_bitcast_fusion.3) | data formatting | bytes 3145728 | tf_op jit(solution)/shard_map/lao,owmc->wlcma/transpose | solution.py:111
  720.4 9.2 all_to_all.85
  735.0 18.4 %convolution_bitcast_fusion.4 = f32[16,32,2,16,24]{1,3,4,2,0:T(8,128)} fusion(f32[32,24,768,1,1]{2,1,0,4,3:T(8,128)} %get-tuple-element.5, f32[768,16,16,1]{0,2,3,1:T(8,128)} %copy-done.7, f32[768,16,16,1]{0,2,3,1:T(8,128)S(1)} %get-tuple-element.13), kind=kOutput, calls=%fused_computation.48 | convolution fusion | flops 3624665088 | bytes 5505024 | tf_op jit(solution)/shard_map/lao,owmc->wlcma/dot_general | solution.py:111
  753.4 10.5 %copy.211 = f32[16,32,2,16,24]{4,3,2,1,0:T(8,128)} copy(f32[16,32,2,16,24]{1,3,4,2,0:T(8,128)} %convolution_bitcast_fusion.4) | data formatting | bytes 3145728 | tf_op jit(solution)/shard_map/lao,owmc->wlcma/transpose | solution.py:111
  763.9 9.1 all_to_all.84
  780.4 18.4 %convolution_bitcast_fusion.2 = f32[16,32,2,16,24]{1,3,4,2,0:T(8,128)} fusion(f32[32,24,768,1,1]{2,1,0,4,3:T(8,128)} %get-tuple-element.7, f32[768,16,16,1]{0,2,3,1:T(8,128)} %copy-done.7, f32[768,16,16,1]{0,2,3,1:T(8,128)S(1)} %get-tuple-element.13), kind=kOutput, calls=%fused_computation.46 | convolution fusion | flops 3624665088 | bytes 5505024 | tf_op jit(solution)/shard_map/lao,owmc->wlcma/dot_general | solution.py:111
  798.9 10.5 %copy.220 = f32[16,32,2,16,24]{4,3,2,1,0:T(8,128)} copy(f32[16,32,2,16,24]{1,3,4,2,0:T(8,128)} %convolution_bitcast_fusion.2) | data formatting | bytes 3145728 | tf_op jit(solution)/shard_map/lao,owmc->wlcma/transpose | solution.py:111
  809.4 9.1 all_to_all.86
  825.1 18.4 %convolution_bitcast_fusion.1 = f32[16,32,2,16,24]{1,3,4,2,0:T(8,128)} fusion(f32[32,24,768,1,1]{2,1,0,4,3:T(8,128)} %get-tuple-element.6, f32[768,16,16,1]{0,2,3,1:T(8,128)} %copy-done.7, f32[768,16,16,1]{0,2,3,1:T(8,128)S(1)} %get-tuple-element.13), kind=kOutput, calls=%fused_computation.45 | convolution fusion | flops 3624665088 | bytes 5505024 | tf_op jit(solution)/shard_map/lao,owmc->wlcma/dot_general | solution.py:111
  843.5 10.5 %copy.224 = f32[16,32,2,16,24]{4,3,2,1,0:T(8,128)} copy(f32[16,32,2,16,24]{1,3,4,2,0:T(8,128)} %convolution_bitcast_fusion.1) | data formatting | bytes 3145728 | tf_op jit(solution)/shard_map/lao,owmc->wlcma/transpose | solution.py:111
  854.0 9.1 all_to_all.87
  883.2 18.7 %fusion.42 = f32[32,16,2,256]{3,0,2,1:T(8,128)S(1)} fusion(f32[16,16,24,256,1]{3,2,1,4,0:T(8,128)} %bitcast.215, f32[16,32,2,16,24]{4,3,2,1,0:T(8,128)} %reshape.356), kind=kOutput, calls=%fused_computation.69 | convolution fusion | flops 1207959552 | bytes 8912896 | tf_op jit(solution)/shard_map/wlcma,mwaj->lmcj/dot_general | solution.py:118
  948.6 18.6 %fusion.39 = f32[1,32,16,2,256]{4,1,3,2,0:T(8,128)S(1)} fusion(f32[16,16,24,256,1]{3,2,1,4,0:T(8,128)} %bitcast.216, f32[16,32,2,16,24]{4,3,2,1,0:T(8,128)} %reshape.355), kind=kOutput, calls=%fused_computation.68 | convolution fusion | flops 1207959552 | bytes 8912896 | tf_op jit(solution)/shard_map/wlcma,mwaj->lmcj/dot_general | solution.py:118
  967.2 20.0 %fusion.45 = f32[1,32,16,2,256]{4,1,3,2,0:T(8,128)} fusion(f32[16,16,24,256,1]{3,2,1,4,0:T(8,128)} %bitcast.217, f32[16,32,2,16,24]{4,3,2,1,0:T(8,128)} %reshape.358), kind=kOutput, calls=%fused_computation.70 | convolution fusion | flops 1207959552 | bytes 8912896 | tf_op jit(solution)/shard_map/wlcma,mwaj->lmcj/dot_general | solution.py:118
  987.3 19.6 %fusion.48 = f32[1,32,16,2,256]{4,1,3,2,0:T(8,128)} fusion(f32[16,16,24,256,1]{3,2,1,4,0:T(8,128)S(1)} %bitcast.220, f32[16,32,2,16,24]{4,3,2,1,0:T(8,128)S(1)} %bitcast.224), kind=kOutput, calls=%fused_computation.71 | convolution fusion | flops 1207959552 | bytes 8912896 | tf_op jit(solution)/shard_map/wlcma,mwaj->lmcj/dot_general | solution.py:118
  (124 shorter events, 239.8 us)
Async XLA Ops:
  6.5 527.1 %copy-start = (bf16[1024,1024]{1,0:T(8,128)(2,1)S(1)}, bf16[1024,1024]{1,0:T(8,128)(2,1)}, u32[]{:S(2)}) copy-start(bf16[1024,1024]{1,0:T(8,128)(2,1)} %param.22) | copy-start | bytes 6291460
  6.5 6.9 copy-start.3
  6.5 0.5 copy-start.11
  14.0 2.6 copy-start.2
  43.7 39.9 %all-to-all-start = ((f32[16,1,24576]{2,1,0:T(1,128)}), f32[16,1,24576]{2,1,0:T(1,128)}, u32[]{:S(2)}, u32[]{:S(2)}) async-start(f32[16,1,24576]{2,1,0:T(1,128)} %all_to_all.80), calls=%async_computation | async-start | bytes 3145728 | tf_op jit(solution)/shard_map/all_to_all | solution.py:84
  83.5 41.0 %all-to-all-start.1 = ((f32[16,1,24576]{2,1,0:T(1,128)}), f32[16,1,24576]{2,1,0:T(1,128)}, u32[]{:S(2)}, u32[]{:S(2)}) async-start(f32[16,1,24576]{2,1,0:T(1,128)} %all_to_all.81), calls=%async_computation.1 | async-start | bytes 3145728 | tf_op jit(solution)/shard_map/all_to_all | solution.py:84
  124.6 41.1 %all-to-all-start.2 = ((f32[16,1,24576]{2,1,0:T(1,128)}), f32[16,1,24576]{2,1,0:T(1,128)}, u32[]{:S(2)}, u32[]{:S(2)}) async-start(f32[16,1,24576]{2,1,0:T(1,128)} %all_to_all.82), calls=%async_computation.2 | async-start | bytes 3145728 | tf_op jit(solution)/shard_map/all_to_all | solution.py:84
  165.6 122.6 %all-to-all-start.3 = ((f32[16,1,24576]{2,1,0:T(1,128)}), f32[16,1,24576]{2,1,0:T(1,128)}, u32[]{:S(2)}, u32[]{:S(2)}) async-start(f32[16,1,24576]{2,1,0:T(1,128)} %all_to_all.83), calls=%async_computation.3 | async-start | bytes 3145728 | tf_op jit(solution)/shard_map/all_to_all | solution.py:84
  174.8 0.6 copy-start.8
  498.9 10.4 %copy-start.13 = (f32[256]{0:T(256)S(1)}, f32[256]{0:T(256)}, u32[]{:S(2)}) copy-start(f32[256]{0:T(256)} %param.19) | copy-start | bytes 3076
  509.3 5.0 copy-start.17
  509.3 5.0 copy-start.19
  514.3 19.4 %copy-start.20 = (f32[1024]{0:T(1024)S(1)}, f32[1024]{0:T(1024)}, u32[]{:S(2)}) copy-start(f32[1024]{0:T(1024)} %param.23) | copy-start | bytes 12292
  533.6 38.6 %copy-start.18 = (bf16[256,1024]{1,0:T(8,128)(2,1)S(1)}, bf16[256,1024]{1,0:T(8,128)(2,1)}, u32[]{:S(2)}) copy-start(bf16[256,1024]{1,0:T(8,128)(2,1)} %param.24) | copy-start | bytes 1572868
  533.6 38.6 %copy-start.21 = (f32[256]{0:T(256)S(1)}, f32[256]{0:T(256)}, u32[]{:S(2)}) copy-start(f32[256]{0:T(256)} %param.25) | copy-start | bytes 3076
  597.3 5.9 copy-start.9
  597.3 58.9 %all-to-all-start.5 = ((bf16[4,64,9216]{2,0,1:T(4,128)(2,1)}), bf16[4,64,9216]{2,0,1:T(4,128)(2,1)}, u32[]{:S(2)}, u32[]{:S(2)}) async-start(bf16[4,64,9216]{2,0,1:T(4,128)(2,1)} %copy.207), calls=%async_computation.5 | async-start | bytes 9437184 | tf_op jit(solution)/shard_map/all_to_all | solution.py:105
  606.5 86.3 %copy-start.7 = (f32[768,16,16,1]{0,2,3,1:T(8,128)}, f32[768,16,16,1]{0,2,3,1:T(8,128)S(1)}, u32[]{:S(2)}) copy-start(f32[768,16,16,1]{0,2,3,1:T(8,128)S(1)} %get-tuple-element.14) | copy-start | bytes 2359300
  669.3 13.1 %copy-start.16 = (f32[24]{0:T(128)S(1)}, f32[24]{0:T(128)}, u32[]{:S(2)}) copy-start(f32[24]{0:T(128)} %param.15) | copy-start | bytes 292
  729.5 43.6 %all-to-all-start.7 = ((f32[16,1,24576]{2,1,0:T(1,128)}), f32[16,1,24576]{2,1,0:T(1,128)S(1)}, u32[]{:S(2)}, u32[]{:S(2)}) async-start(f32[16,1,24576]{2,1,0:T(1,128)} %all_to_all.85), calls=%async_computation.7 | async-start | bytes 3145728 | tf_op jit(solution)/shard_map/all_to_all | solution.py:114
  773.1 1.1 copy-start.5
  774.2 44.3 %all-to-all-start.6 = ((f32[16,1,24576]{2,1,0:T(1,128)}), f32[16,1,24576]{2,1,0:T(1,128)S(1)}, u32[]{:S(2)}, u32[]{:S(2)}) async-start(f32[16,1,24576]{2,1,0:T(1,128)} %all_to_all.84), calls=%async_computation.6 | async-start | bytes 3145728 | tf_op jit(solution)/shard_map/all_to_all | solution.py:114
  818.5 25.0 %copy-start.4 = (f32[16,1,24576]{2,1,0:T(1,128)}, f32[16,1,24576]{2,1,0:T(1,128)S(1)}, u32[]{:S(2)}) copy-start(f32[16,1,24576]{2,1,0:T(1,128)S(1)} %all-to-all-done.6) | copy-start | bytes 4718596
  818.5 44.7 %all-to-all-start.8 = ((f32[16,1,24576]{2,1,0:T(1,128)}), f32[16,1,24576]{2,1,0:T(1,128)}, u32[]{:S(2)}, u32[]{:S(2)}) async-start(f32[16,1,24576]{2,1,0:T(1,128)} %all_to_all.86), calls=%async_computation.8 | async-start | bytes 3145728 | tf_op jit(solution)/shard_map/all_to_all | solution.py:114
  854.0 15.4 %copy-start.12 = (s32[16]{0:T(128)S(1)}, s32[16]{0:T(128)}, u32[]{:S(2)}) copy-start(s32[16]{0:T(128)} %copy-done.11) | copy-start | bytes 196
  854.0 15.5 %copy-start.14 = (f32[64]{0:T(128)S(1)}, f32[64]{0:T(128)}, u32[]{:S(2)}) copy-start(f32[64]{0:T(128)} %param.17) | copy-start | bytes 772
  863.2 71.9 %all-to-all-start.9 = ((f32[16,1,24576]{2,1,0:T(1,128)}), f32[16,1,24576]{2,1,0:T(1,128)}, u32[]{:S(2)}, u32[]{:S(2)}) async-start(f32[16,1,24576]{2,1,0:T(1,128)} %all_to_all.87), calls=%async_computation.9 | async-start | bytes 3145728 | tf_op jit(solution)/shard_map/all_to_all | solution.py:114
  869.3 137.6 %all-gather.2.cloned.1.call-start = ((), (), s32[]{:S(2)}) async-start(), calls=%async_computation.10 | async-start | bytes 3145728 | tf_op jit(solution)/shard_map/all_gather | solution.py:128
  901.9 2.8 copy-start.15
  948.6 38.7 %slice-start = ((s8[6291456]{0:T(1024)(128)(4,1)}), s8[4194304]{0:T(1024)(128)(4,1)S(1)}, s32[]{:S(2)}) async-start(s8[6291456]{0:T(1024)(128)(4,1)} %bitcast.218), calls=%async_computation.11 | async-start | bytes 8388608
  948.6 38.7 %slice-start.2 = ((s8[8388608]{0:T(1024)(128)(4,1)}), s8[4194304]{0:T(1024)(128)(4,1)S(1)}, s32[]{:S(2)}) async-start(s8[8388608]{0:T(1024)(128)(4,1)} %bitcast.223), calls=%async_computation.13 | async-start | bytes 8388608
  967.2 20.1 %slice-start.1 = ((s8[6291456]{0:T(1024)(128)(4,1)}), s8[2097152]{0:T(1024)(128)(4,1)S(1)}, s32[]{:S(2)}) async-start(s8[6291456]{0:T(1024)(128)(4,1)} %bitcast.218), calls=%async_computation.12 | async-start | bytes 4194304
  967.2 20.1 %slice-start.3 = ((s8[8388608]{0:T(1024)(128)(4,1)}), s8[4194304]{0:T(1024)(128)(4,1)S(1)}, s32[]{:S(2)}) async-start(s8[8388608]{0:T(1024)(128)(4,1)} %bitcast.223), calls=%async_computation.14 | async-start | bytes 8388608
  987.3 19.6 %copy-start.6 = (f32[64,8192]{1,0:T(8,128)S(1)}, f32[64,8192]{1,0:T(8,128)}, u32[]{:S(2)}) copy-start(f32[64,8192]{1,0:T(8,128)} %reshape.357) | copy-start | bytes 6291460
  987.3 19.6 %copy-start.10 = (f32[64,64]{1,0:T(8,128)S(1)}, f32[64,64]{1,0:T(8,128)}, u32[]{:S(2)}) copy-start(f32[64,64]{1,0:T(8,128)} %param.16) | copy-start | bytes 49156
  1013.2 7.8 copy-start.1
Sparse Core Ops, SparseCore 0:
  904.7 33.4 all-gather.1
where the time goes:
time: 1040 us; the launch traced here: 1030 us
  local copies, waits for them, and re-layouts  411 us (40%)
  matrix products  342 us (33%)
  other arithmetic  77.7 us (7%)
  starting transfers between devices  65.8 us (6%)
  blocking collectives  61.8 us (6%)
  waiting for transfers between devices  55 us (5%)
  between operations  14.2 us (1%)
    dot_general x4, matrix products, body(): jnp.einsum('wlcma,mwaj->lmcj', shaped, basis_blocks, precision=highest)  76.9 us
    dot_general x4, matrix products, body(): jnp.einsum('lao,owmc->wlcma', updated[field_index], forward_tab, precisio...  72.3 us
    dot_general x4, matrix products, body(): jnp.einsum('wlcma,wmco->lao', shaped, inverse_tab, precision=highest)  71.6 us
    reshape x8, local copies, waits for them, and re-layouts, body(): exchanged.reshape(wave_count, lev_dev, complex_parts, m_dev, lat_dev)  70.3 us
    all_to_all x1, blocking collectives, body(): lax.all_to_all(slab, 'level', split_axis=2, concat_axis=1, tiled=True)  61.8 us
    unnamed x54, local copies, waits for them, and re-layouts  53.4 us
    all_to_all x1, waiting for transfers between devices, body(): lax.all_to_all(tendency, 'level', split_axis=1, concat_axis=2, tiled=True)  49.7 us
    transpose x4, local copies, waits for them, and re-layouts, body(): jnp.einsum('lao,owmc->wlcma', updated[field_index], forward_tab, precisio...  42.1 us
  transfers between devices with their start and end apart: 10, of which 4 were waited for; matrix products, arithmetic and copies ran while one was open for 39% of the time, Pallas kernels for 0%

commit v1 on v0

v1 whole, which is shorter than its diff:
```python
import functools

import jax
import jax.numpy as jnp
from jax import lax
from jax.experimental import pallas as pl
from jax.experimental.pallas import tpu as pltpu
from jax.sharding import PartitionSpec as P

high = lax.Precision.HIGH
norm_eps = 1e-06
axes = ("wave", "level")
send_scale = 1024.0


def phase_angles(waves, longitudes):
    wave_idx = jnp.arange(waves, dtype=jnp.int32)
    lon_idx = jnp.arange(longitudes, dtype=jnp.int32)
    phase_turns = wave_idx[:, None] * lon_idx[None, :] % longitudes
    return (2.0 * jnp.pi / longitudes * phase_turns.astype(jnp.float32), wave_idx)


def synthesis_table(waves, longitudes):
    angle_table, wave_idx = phase_angles(waves, longitudes)
    factor = jnp.where(wave_idx == 0, 1.0, 2.0).astype(jnp.float32)[:, None]
    return jnp.stack([factor * jnp.cos(angle_table), -factor * jnp.sin(angle_table)], axis=1)


def analysis_table(waves, longitudes):
    angle_table, _ = phase_angles(waves, longitudes)
    return jnp.stack([jnp.cos(angle_table), -jnp.sin(angle_table)], axis=1) / longitudes


def contract_last(left, right):
    return lax.dot_general(
        left, right, (((1,), (1,)), ((), ())), preferred_element_type=jnp.float32
    )


def physics_kernel(grid_ref, lat_ref, gain_ref, w1_ref, b1_ref, w2_ref, b2_ref, w3_ref, b3_ref, out_ref, top_ref):
    grid_rows = grid_ref[0]
    values = grid_rows.astype(jnp.bfloat16).astype(jnp.float32)
    inverse_rms = lax.rsqrt(jnp.mean(values * values, axis=1, keepdims=True) + norm_eps)
    normed = (values * inverse_rms * gain_ref[...]).astype(jnp.bfloat16)
    hidden = jax.nn.gelu(contract_last(normed, w1_ref[...]) + b1_ref[...]).astype(jnp.bfloat16)
    hidden = jax.nn.gelu(contract_last(hidden, w2_ref[...]) + b2_ref[...]).astype(jnp.bfloat16)
    tendency = (contract_last(hidden, w3_ref[...]) + b3_ref[...]).astype(jnp.bfloat16)
    updated = (grid_rows + tendency.astype(jnp.float32)) * lat_ref[pl.program_id(0)]
    out_ref[0] = updated
    top_ref[0] = jnp.max(jnp.abs(updated), axis=0, keepdims=True)


def column_step(grid, lat, gain, w1, b1, w2, b2, w3, b3):
    rows, lon, feats = grid.shape
    hid = w1.shape[0]
    whole = lambda *shape: pl.BlockSpec(shape, lambda i: (0,) * len(shape))
    block = pl.BlockSpec((1, lon, feats), lambda i: (i, 0, 0))
    return pl.pallas_call(
        physics_kernel,
        grid=(rows,),
        out_shape=(
            jax.ShapeDtypeStruct((rows, lon, feats), jnp.float32),
            jax.ShapeDtypeStruct((rows, 1, feats), jnp.float32),
        ),
        in_specs=[
            block,
            pl.BlockSpec(memory_space=pltpu.SMEM),
            whole(1, feats),
            whole(hid, feats),
            whole(1, hid),
            whole(hid, hid),
            whole(1, hid),
            whole(feats, hid),
            whole(1, feats),
        ],
        out_specs=(block, pl.BlockSpec((1, 1, feats), lambda i: (i, 0, 0))),
        compiler_params=pltpu.CompilerParams(vmem_limit_bytes=56 * 1024 * 1024),
    )(grid, lat, gain[None], w1, b1[None], w2, b2[None], w3, b3[None])


def body(
    longitudes,
    state,
    legendre,
    lat_weight,
    modes,
    mode_rates,
    diffusion,
    norm_gain,
    w_first,
    b_first,
    w_second,
    b_second,
    w_third,
    b_third,
):
    fields, lev_dev, m_dev, parts, degrees = state.shape
    levels = modes.shape[0]
    waves = degrees
    wave_count = lax.axis_size("wave")
    level_count = lax.axis_size("level")
    lat_band = lat_weight.shape[0]
    lat_own = -(-lat_band // level_count)
    lat_extra = lat_own * level_count - lat_band
    wave_global = lax.axis_index("wave") * m_dev + jnp.arange(m_dev, dtype=jnp.int32)
    degree_index = wave_global[:, None] + jnp.arange(degrees, dtype=jnp.int32)[None, :]
    kept_mask = (degree_index < waves).astype(jnp.float32)
    basis = legendre * kept_mask[:, None, :]
    if lat_extra:
        basis = basis.reshape(m_dev, wave_count, lat_band, degrees)
        basis = jnp.pad(basis, ((0, 0), (0, 0), (0, lat_extra), (0, 0)))
        basis = basis.reshape(m_dev, -1, degrees)
        lat_weight = jnp.pad(lat_weight, (0, lat_extra))
    inverse_tab = synthesis_table(waves, longitudes).reshape(wave_count, m_dev, parts, longitudes)
    forward_tab = analysis_table(waves, longitudes).reshape(wave_count, m_dev, parts, longitudes)

    band = jnp.einsum("flmcj,maj->amcfl", state, basis, precision=high)
    band = (band * send_scale).astype(jnp.float16)
    band = band.reshape(wave_count * level_count, lat_own, m_dev, parts, fields, lev_dev)
    band = lax.all_to_all(band, axes, split_axis=0, concat_axis=0, tiled=True)
    band = band.reshape(wave_count, level_count, lat_own, m_dev, parts, fields, lev_dev)
    band = band.astype(jnp.float32) * (1.0 / send_scale)
    grid = jnp.einsum("wvamcfl,wmco->aovfl", band, inverse_tab, precision=high)
    feats = fields * levels
    grid = grid.reshape(lat_own, longitudes, feats)

    def slabs_first(x):
        split = x.reshape((fields, level_count, lev_dev) + x.shape[1:])
        return jnp.swapaxes(split, 0, 1).reshape(x.shape)

    lat = lax.dynamic_slice_in_dim(lat_weight, lax.axis_index("level") * lat_own, lat_own, 0)
    updated, tops = column_step(
        grid,
        lat,
        slabs_first(norm_gain),
        slabs_first(w_first.T).T,
        b_first,
        w_second,
        b_second,
        slabs_first(w_third),
        slabs_first(b_third),
    )
    top = jnp.maximum(jnp.max(tops), 1e-25)
    reach = 32768.0 / levels**0.5
    tops_all = lax.all_gather(top / reach, axes).reshape(wave_count, level_count)

    wave = jnp.einsum("aok,wmco->wmcak", updated, forward_tab, precision=high)
    wave = wave * (reach / top)
    wave = wave.reshape(wave_count, m_dev, parts, lat_own, level_count, fields, lev_dev)
    modal = jnp.einsum(
        "wmcavl,vlk->wmcak",
        wave[..., 1, :],
        modes.reshape(level_count, lev_dev, levels),
        precision=high,
    )
    others = jnp.concatenate([wave[..., :1, :], wave[..., 2:, :]], axis=-2)
    others = others.reshape(wave_count, m_dev, parts, lat_own, level_count, (fields - 1) * lev_dev)
    others = jnp.moveaxis(others, 4, 1)
    modal = jnp.broadcast_to(modal[:, None], others.shape[:-1] + (levels,))
    sent = jnp.concatenate([others, modal], axis=-1).astype(jnp.float16)
    sent = sent.reshape((wave_count * level_count,) + sent.shape[2:])
    got = lax.all_to_all(sent, axes, split_axis=0, concat_axis=0, tiled=True)
    got = got.reshape((wave_count, level_count) + got.shape[1:]).astype(jnp.float32)
    got = got * tops_all[:, :, None, None, None, None]
    basis_split = basis.reshape(m_dev, wave_count, level_count, lat_own, degrees)
    spectral = jnp.einsum("wvmcaq,mwvaj->qmcj", got, basis_split, precision=high)

    growth = (degree_index * (degree_index + 1)).astype(jnp.float32)
    plain = spectral[: (fields - 1) * lev_dev].reshape(fields - 1, lev_dev, m_dev, parts, degrees)
    divisor = 1.0 + mode_rates[:, None, None, None] * growth[None, :, None, :]
    amplitude = spectral[(fields - 1) * lev_dev :] / divisor
    own_rows = lax.dynamic_slice_in_dim(modes, lax.axis_index("level") * lev_dev, lev_dev, 0)
    solved = jnp.einsum("lk,kmcj->lmcj", own_rows, amplitude, precision=high)
    combined = jnp.concatenate([plain[:1], solved[None], plain[1:]], axis=0)
    scaled_growth = growth / (waves * (waves - 1))
    damping = 1.0 + diffusion[:, None, None] * (scaled_growth * scaled_growth)[None]
    return combined / damping[:, None, :, None, :]


def solution(mesh):
    def step(state, legendre, *rest):
        longitudes = 2 * legendre.shape[1]
        mapped = jax.shard_map(
            functools.partial(body, longitudes),
            mesh=mesh,
            in_specs=(P(None, "level", "wave", None, None), P("wave", None, None), P("wave")) + (P(),) * 10,
            out_specs=P(None, "level", "wave", None, None),
            check_vma=False,
        )
        return mapped(state, legendre, *rest)

    return step
```

time: 1040 us -> 623 us (0.60)
  local copies, waits for them, and re-layouts: 411 us -> 154 us
  matrix products: 342 us -> 109 us
  blocking collectives: 61.8 us -> 150 us
  starting transfers between devices: 65.8 us -> 11.3 us
  Pallas kernels: 0 us -> 43.4 us
  between operations: 14.2 us -> 1.35 us
  other arithmetic: 77.7 us -> 89.5 us
    dot_general x21 -> x6, matrix products: 342 us -> 109 us  [the longest x1 51.2 us: body(): grid = jnp.einsum('wvamcfl,wmco->aovfl', band, inverse_tab, precision=high)]
    unnamed x0 -> x1, blocking collectives: none -> 150 us
    all_to_all x10 -> x0, local copies, waits for them, and re-layouts: 99.7 us -> none  [the longest x4 36.6 us: body(): lax.all_to_all(wave_coeffs.reshape(wave_count, -1), 'wave', split_axis=0,...]
    transpose x9 -> x5, local copies, waits for them, and re-layouts: 84.1 us -> 11.3 us  [the longest x1 8.52 us: body(): grid = jnp.einsum('wvamcfl,wmco->aovfl', band, inverse_tab, precision=high)]
    all_to_all x1 -> x0, blocking collectives: 61.8 us -> none  [body(): lax.all_to_all(slab, 'level', split_axis=2, concat_axis=1, tiled=True)]
    all_to_all x9 -> x2, starting transfers between devices: 65.7 us -> 11.3 us  [the longest x1 7.59 us: body(): band = lax.all_to_all(band, axes, split_axis=0, concat_axis=0, tiled=True)]
    all_to_all x8 -> x0, other arithmetic: 46.2 us -> none  [the longest x4 25.4 us: body(): lax.all_to_all(band_coeffs.reshape(wave_count, -1), 'wave', split_axis=0,...]
    pallas_call x0 -> x1, Pallas kernels: none -> 43.4 us  [column_step(): pl.pallas_call(physics_kernel, grid=(rows,), out_shape=(jax.ShapeDtypeStr...]
  transfers between devices with their start and end apart: 10 -> 2, of which waited for: 4 -> 1; matrix products, arithmetic and copies ran while one was open for 39% -> 4% of each run, Pallas kernels for 0% -> 0%
where the time goes in v1:
time: 623 us; the launch traced here: 613 us
  local copies, waits for them, and re-layouts  154 us (25%)
  blocking collectives  150 us (24%)
  matrix products  109 us (17%)
  other arithmetic  89.5 us (14%)
  waiting for transfers between devices  55.5 us (9%)
  Pallas kernels  43.4 us (7%)
  starting transfers between devices  11.3 us (2%)
    unnamed x1, blocking collectives  150 us
    all_to_all x1, waiting for transfers between devices, body(): band = lax.all_to_all(band, axes, split_axis=0, concat_axis=0, tiled=True)  55.5 us
    dot_general x1, matrix products, body(): grid = jnp.einsum('wvamcfl,wmco->aovfl', band, inverse_tab, precision=high)  51.2 us
    pallas_call x1, Pallas kernels, column_step(): pl.pallas_call(physics_kernel, grid=(rows,), out_shape=(jax.ShapeDtypeStr...  43.4 us
    unnamed x31, local copies, waits for them, and re-layouts  31.8 us
    dot_general x1, matrix products, body(): jnp.einsum('wvmcaq,mwvaj->qmcj', got, basis_split, precision=high)  29.3 us
    convert_element_type x1, local copies, waits for them, and re-layouts, body(): band = (band * send_scale).astype(jnp.float16)  21.9 us
    concatenate x1, other arithmetic, body(): others = jnp.concatenate([wave[..., :1, :], wave[..., 2:, :]], axis=-2)  20.7 us
  transfers between devices with their start and end apart: 2, of which 1 were waited for; matrix products, arithmetic and copies ran while one was open for 4% of the time, Pallas kernels for 0%

profile of v1, /device:TPU:0, one launch (start us, length us, event | category | flops | bytes accessed | tf_op | source)
XLA Modules:
  0.0 613.5 jit_solution(5170881032946603043)
XLA Ops:
  0.1 6.6 %fusion.51 = f32[16,384,256,1,1]{2,0,1,4,3:T(8,128)S(1)} fusion(f32[16,256]{1,0:T(8,128)S(1)} %fusion.46, f32[16,384,256]{2,1,0:T(8,128)} %param.14), kind=kLoop, calls=%fused_computation.64 | loop fusion | flops 1572864 | bytes 12599296 | tf_op jit(solution)/shard_map/mul | solution.py:108
  6.7 8.9 %fusion.14 = f16[384,16,2,4,32]{0,4,2,3,1:T(8,128)(2,1)S(1)} fusion(f32[4,32,16,2,256]{4,3,2,1,0:T(2,128)S(1)} %copy-done.2, f32[16,384,256,1,1]{2,0,1,4,3:T(8,128)S(1)} %fusion.51), kind=kOutput, calls=%fused_computation.21 | convolution fusion | flops 2419064832 | bytes 13631488 | tf_op jit(solution)/shard_map/flmcj,maj->amcfl/dot_general | solution.py:117
  15.6 21.9 %copy.29 = f16[384,16,2,4,32]{4,1,3,2,0:T(8,128)(2,1)} copy(f16[384,16,2,4,32]{0,4,2,3,1:T(8,128)(2,1)S(1)} %fusion.14) | data formatting | bytes 6291456 | tf_op jit(solution)/shard_map/convert_element_type | solution.py:118
  37.4 17.7 %reshape.288 = f16[32,2,24576]{2,1,0:T(2,128)(2,1)} reshape(f16[32,12,2,4,16,32]{5,4,3,2,1,0:T(8,128)(2,1)} %bitcast.91) | data formatting | bytes 6291456
  55.2 7.6 %all-to-all-start = ((f16[32,2,24576]{2,1,0:T(2,128)(2,1)}), f16[32,2,24576]{2,1,0:T(2,128)(2,1)S(1)}, u32[]{:S(2)}, u32[]{:S(2)}) async-start(f16[32,2,24576]{2,1,0:T(2,128)(2,1)} %reshape.288), calls=%async_computation | async-start | bytes 6291456 | tf_op jit(solution)/shard_map/all_to_all | solution.py:120
  62.9 0.7 broadcast_in_dim_reshape.7.gain_ref
  63.6 2.0 copy.33
  65.6 1.9 copy.34
  67.5 2.1 copy.35
  69.5 1.9 copy.36
  71.5 0.7 broadcast_in_dim_reshape.8.b3_ref
  72.2 0.6 dynamic_slice.6.lat_ref
  72.8 4.4 fusion.38
  77.2 1.3 fusion.27
  78.5 55.5 %all-to-all-done = f16[32,2,24576]{2,1,0:T(2,128)(2,1)S(1)} async-done(((f16[32,2,24576]{2,1,0:T(2,128)(2,1)}), f16[32,2,24576]{2,1,0:T(2,128)(2,1)S(1)}, u32[]{:S(2)}, u32[]{:S(2)}) %all-to-all-start) | async-done | bytes 3145760 | tf_op jit(solution)/shard_map/all_to_all | solution.py:120
  134.0 11.9 %reshape.289 = f16[32,12,2,4,16,32]{5,4,3,2,1,0:T(8,128)(2,1)} reshape(f16[32,2,24576]{2,1,0:T(2,128)(2,1)S(1)} %all-to-all-done) | data formatting | bytes 6291456
  145.9 14.7 %convert_multiply_fusion = f32[32,12,16,2,4,32]{5,2,4,3,1,0:T(8,128)} fusion(f16[32,12,2,4,16,32]{5,4,3,2,1,0:T(8,128)(2,1)} %reshape.289), kind=kLoop, calls=%fused_computation.3 | loop fusion | flops 3145728 | bytes 9437184 | tf_op jit(solution)/shard_map/mul | solution.py:122
  160.6 51.2 %fusion.11 = f32[12,768,2,4,32]{1,4,3,0,2:T(8,128)} fusion(f32[16,2,12,16,2,4,32]{6,3,5,4,2,1,0:T(8,128)} %bitcast.93, f32[16,16,1,768]{3,0,1,2:T(8,128)S(1)} %copy-done.6, f32[16,16,1,768]{3,0,1,2:T(8,128)S(1)} %copy-done.7), kind=kOutput, calls=%fused_computation.20 | convolution fusion | flops 7248150528 | bytes 17301504 | tf_op jit(solution)/shard_map/wvamcfl,wmco->aovfl/dot_general | solution.py:123
  211.8 8.5 %copy.31 = f32[12,768,2,4,32]{1,4,3,2,0:T(8,128)} copy(f32[12,768,2,4,32]{1,4,3,0,2:T(8,128)} %fusion.11) | data formatting | bytes 18874368 | tf_op jit(solution)/shard_map/wvamcfl,wmco->aovfl/transpose | solution.py:123
  220.3 9.6 %copy.38.grid_ref = f32[12,768,256]{2,1,0:T(8,128)} copy(f32[12,768,256]{1,2,0:T(8,128)} %bitcast.92) | data formatting | bytes 18874368 | tf_op jit(solution)/shard_map/reshape | solution.py:125
  229.9 43.4 %shard_map.127 = (f32[12,768,256]{2,1,0:T(8,128)}, f32[12,1,256]{2,1,0:T(1,128)}) custom-call(f32[12,768,256]{2,1,0:T(8,128)} %copy.38.grid_ref, f32[12]{0:T(128)} %dynamic_slice.6.lat_ref, f32[1,256]{1,0:T(1,128)} %broadcast_in_dim_reshape.7.gain_ref, bf16[1024,256]{1,0:T(8,128)(2,1)} %bitcast.99, f32[1,1024]{1,0:T(1,128)} %bitcast.106, ...), custom_call_target="tpu_custom_call" | custom-call | tf_op jit(solution)/shard_map/pallas_call | solution.py:58
  273.3 1.4 reduce_max.9
  275.4 13.4 %broadcast_multiply_fusion = f32[16,16,2,12,256]{4,1,3,2,0:T(8,128)} fusion(f32[]{:T(128)S(6)} %div.36, f32[12,768,256]{2,1,0:T(8,128)} %get-tuple-element.7, f32[16,16,2,768,1]{3,0,1,2,4:T(8,128)S(1)} %copy-done.4), kind=kOutput, calls=%fused_computation.23 | convolution fusion | flops 7249330176 | bytes 17301508 | tf_op jit(solution)/shard_map/aok,wmco->wmcak/dot_general | solution.py:147
  288.8 18.4 %reshape.272 = f32[16,16,2,12,2,4,32]{6,5,4,1,3,2,0:T(4,128)} reshape(f32[16,16,2,12,256]{4,1,3,2,0:T(8,128)} %broadcast_multiply_fusion) | data formatting | bytes 12582912 | tf_op jit(solution)/shard_map/reshape | solution.py:149
  307.2 12.5 %slice.39 = f32[16,16,2,12,2,1,32]{6,5,4,1,3,2,0:T(1,128)} slice(f32[16,16,2,12,2,4,32]{6,5,4,1,3,2,0:T(4,128)} %reshape.272), slice={[0:16], [0:16], [0:2], [0:12], [0:2], [1:2], [0:32]} | slice | bytes 3145728 | tf_op jit(solution)/shard_map/slice | solution.py:152
  319.7 10.6 %copy_convert_fusion = f16[16,16,2,12,2,4,32]{6,5,1,4,3,2,0:T(4,128)(2,1)S(1)} fusion(f32[16,16,2,12,2,4,32]{6,5,4,1,3,2,0:T(4,128)} %reshape.272), kind=kLoop, calls=%fused_computation | loop fusion | flops 1572864 | bytes 9437184 | tf_op jit(solution)/shard_map/convert.10 | solution.py:190
  330.4 8.4 %slice.38 = f16[16,16,2,12,2,2,32]{6,5,1,4,3,2,0:T(2,128)(2,1)S(1)} slice(f16[16,16,2,12,2,4,32]{6,5,1,4,3,2,0:T(4,128)(2,1)S(1)} %copy_convert_fusion), slice={[0:16], [0:16], [0:2], [0:12], [0:2], [2:4], [0:32]} | slice | bytes 3145728 | tf_op jit(solution)/shard_map/slice | solution.py:156
  338.8 7.2 %slice.37 = f16[16,16,2,12,2,1,32]{6,5,1,4,3,2,0:T(2,128)(2,1)S(1)} slice(f16[16,16,2,12,2,4,32]{6,5,1,4,3,2,0:T(4,128)(2,1)S(1)} %copy_convert_fusion), slice={[0:16], [0:16], [0:2], [0:12], [0:2], [0:1], [0:32]} | slice | bytes 1572864 | tf_op jit(solution)/shard_map/slice | solution.py:156
  346.0 20.7 %pad_maximum_fusion = f16[16,16,2,12,2,3,32]{6,5,1,4,3,2,0:T(4,128)(2,1)} fusion(f16[16,16,2,12,2,2,32]{6,5,1,4,3,2,0:T(2,128)(2,1)S(1)} %slice.38, f16[16,16,2,12,2,1,32]{6,5,1,4,3,2,0:T(2,128)(2,1)S(1)} %slice.37), kind=kLoop, calls=%fused_computation.4 | loop fusion | flops 1179648 | bytes 4718592 | tf_op jit(solution)/shard_map/concatenate | solution.py:156
  366.8 20.1 %reshape.273 = f16[16,16,2,12,2,96]{5,1,4,3,2,0:T(8,128)(2,1)S(1)} reshape(f16[16,16,2,12,2,3,32]{6,5,1,4,3,2,0:T(4,128)(2,1)} %pad_maximum_fusion) | data formatting | bytes 4718592 | tf_op jit(solution)/shard_map/reshape | solution.py:157
  386.9 0.9 copy.41
  387.8 5.4 bitcast_convert_fusion
  393.2 0.8 broadcast_in_dim.20
  394.0 6.2 %pad_maximum_fusion.1 = f16[32,16,2,12,160]{4,1,3,2,0:T(8,128)(2,1)} fusion(f16[32,16,2,12,64]{4,1,3,2,0:T(8,128)(2,1)S(1)} %bitcast.97, f16[32,16,2,12,96]{4,1,3,2,0:T(8,128)(2,1)S(1)} %bitcast.96), kind=kLoop, calls=%fused_computation.10 | loop fusion | flops 1966080 | bytes 7864320 | tf_op jit(solution)/shard_map/concatenate | solution.py:160
  400.2 3.7 all-to-all-start.1
  404.2 1.1 multiply_add_fusion
  405.3 9.1 %copy_multiply_fusion = f32[16,384,256]{2,0,1:T(8,128)} fusion(f32[16,384,256]{2,1,0:T(8,128)} %param.14, f32[16,256]{1,0:T(8,128)S(1)} %fusion.46), kind=kLoop, calls=%fused_computation.16 | loop fusion | flops 1572864 | bytes 12599296 | tf_op jit(solution)/shard_map/mul | solution.py:108
  414.4 0.1 dynamic-update-slice
  414.5 150.0 %all-reduce = f32[32]{0:T(128)S(1)} all-reduce(f32[32]{0:T(128)S(1)} %dynamic-update-slice), channel_id=1, replica_groups=mesh['wave'=16,'level'=2] {'wave','level'}, use_global_device_ids=true, to_apply=%add | all-reduce | flops 32 | bytes 256
  564.6 9.4 %convert_multiply_fusion.1 = f32[16,2,16,2,12,160]{5,2,4,3,1,0:T(8,128)} fusion(f16[16,2,16,2,12,160]{5,2,4,3,1,0:T(8,128)(2,1)} %bitcast.58, f32[16,2]{1,0:T(8,128)S(1)} %mul.288), kind=kLoop, calls=%fused_computation.5 | loop fusion | flops 3932160 | bytes 11796608 | tf_op jit(solution)/shard_map/mul | solution.py:164
  574.0 29.3 %fusion.17 = f32[160,16,2,256]{3,0,2,1:T(8,128)} fusion(f32[16,2,16,2,12,160]{5,2,4,3,1,0:T(8,128)} %convert_multiply_fusion.1, f32[16,16,2,12,256,1]{4,0,3,2,1,5:T(8,128)S(1)} %bitcast.94), kind=kOutput, calls=%fused_computation.24 | convolution fusion | flops 3019898880 | bytes 19398656 | tf_op jit(solution)/shard_map/wvmcaq,mwvaj->qmcj/dot_general | solution.py:166
  603.3 1.5 slice_bitcast_fusion
  604.8 0.4 slice-done
  605.2 1.9 copy.47
  607.1 0.7 fusion.31
  607.8 0.8 copy.46
  608.6 0.8 copy.45
  609.4 3.6 maximum_divide_fusion
  (41 shorter events, 0.6 us)
Async XLA Ops:
  0.0 387.8 %copy-start = (f32[64,64]{1,0:T(8,128)S(1)}, f32[64,64]{1,0:T(8,128)}, u32[]{:S(2)}) copy-start(f32[64,64]{1,0:T(8,128)} %param.16) | copy-start | bytes 49156
  0.1 6.6 %copy-start.2 = (f32[4,32,16,2,256]{4,3,2,1,0:T(2,128)S(1)}, f32[4,32,16,2,256]{4,3,2,1,0:T(2,128)}, u32[]{:S(2)}) copy-start(f32[4,32,16,2,256]{4,3,2,1,0:T(2,128)} %param.13) | copy-start | bytes 12582916
  55.2 7.6 %copy-start.8 = (f32[256]{0:T(256)S(1)}, f32[256]{0:T(256)}, u32[]{:S(2)}) copy-start(f32[256]{0:T(256)} %param.19) | copy-start | bytes 3076
  55.2 16.2 %copy-start.9 = (f32[256]{0:T(256)S(1)}, f32[256]{0:T(256)}, u32[]{:S(2)}) copy-start(f32[256]{0:T(256)} %param.25) | copy-start | bytes 3076
  55.2 17.0 %copy-start.12 = (f32[24]{0:T(128)S(1)}, f32[24]{0:T(128)}, u32[]{:S(2)}) copy-start(f32[24]{0:T(128)} %param.15) | copy-start | bytes 292
  55.2 78.8 %all-to-all-start = ((f16[32,2,24576]{2,1,0:T(2,128)(2,1)}), f16[32,2,24576]{2,1,0:T(2,128)(2,1)S(1)}, u32[]{:S(2)}, u32[]{:S(2)}) async-start(f16[32,2,24576]{2,1,0:T(2,128)(2,1)} %reshape.288), calls=%async_computation | async-start | bytes 6291456 | tf_op jit(solution)/shard_map/all_to_all | solution.py:120
  145.9 14.7 %copy-start.6 = (f32[16,16,1,768]{3,0,1,2:T(8,128)S(1)}, f32[16,16,1,768]{3,0,1,2:T(8,128)}, u32[]{:S(2)}) copy-start(f32[16,16,1,768]{3,0,1,2:T(8,128)} %get-tuple-element.10) | copy-start | bytes 2359300
  145.9 14.7 %copy-start.7 = (f32[16,16,1,768]{3,0,1,2:T(8,128)S(1)}, f32[16,16,1,768]{3,0,1,2:T(8,128)}, u32[]{:S(2)}) copy-start(f32[16,16,1,768]{3,0,1,2:T(8,128)} %get-tuple-element.12) | copy-start | bytes 2359300
  229.9 45.5 %copy-start.4 = (f32[16,16,2,768,1]{3,0,1,2,4:T(8,128)S(1)}, f32[16,16,2,768,1]{3,0,1,2,4:T(8,128)}, u32[]{:S(2)}) copy-start(f32[16,16,2,768,1]{3,0,1,2,4:T(8,128)} %fusion.27) | copy-start | bytes 4718596
  400.2 3.9 copy-start.10
  400.2 4.0 copy-start.11
  400.2 164.4 %all-to-all-start.1 = ((f16[32,16,2,12,160]{4,1,3,2,0:T(8,128)(2,1)}), f16[32,16,2,12,160]{4,1,3,2,0:T(8,128)(2,1)}, u32[]{:S(2)}, u32[]{:S(2)}) async-start(f16[32,16,2,12,160]{4,1,3,2,0:T(8,128)(2,1)} %pad_maximum_fusion.1), calls=%async_computation.1 | async-start | bytes 12582912 | tf_op jit(solution)/shard_map/all_to_all | solution.py:162
  564.6 9.4 %copy-start.1 = (f32[16,384,256]{2,0,1:T(8,128)S(1)}, f32[16,384,256]{2,0,1:T(8,128)}, u32[]{:S(2)}) copy-start(f32[16,384,256]{2,0,1:T(8,128)} %copy_multiply_fusion) | copy-start | bytes 18874372
  603.3 1.9 slice-start
  603.3 3.8 copy-start.3
  603.3 3.8 copy-start.5
